TPU v7x, 32 devices: a whole 2x2x4 slice. The times are simulated.
32 devices in a mesh: frame: 8 (over y, x, core), tensor: 4 (over z).
Axes of the slice: x: 2, y: 2, z: 4, core: 2. Of those that a mesh axis runs over, the one named last changes fastest.
Arguments:
- tokens: bfloat16 [1024, 1, 4096], P(('frame', 'tensor')), may hold values from -6 to 6
- norm_gain: float32 [4096], replicated, may hold values from 0.5 to 1.5
- query_weight: bfloat16 [4096, 4096], P(None, 'tensor'), may hold values from -0.09375 to 0.09375
- out_weight: bfloat16 [4096, 4096], P('tensor'), may hold values from -0.09375 to 0.09375
- cache_keys: bfloat16 [384, 1, 4096], P('frame', None, 'tensor'), may hold values from -420 to 420
- cache_values: bfloat16 [384, 1, 4096], P('frame', None, 'tensor'), may hold values from -18 to 18
- token_pos: int32 [1024, 1], P('frame'), may hold values from 0 to 383, as said below
- frame_pad: int32 [1], replicated, may hold values from 0 to 192
Outputs:
- mixed: bfloat16 [1024, 1, 4096], P(('frame', 'tensor'))
Inputs may be any that keep to these rules, and one draw needn't show every extreme that they name: `token_pos`: nondecreasing along each sequence; the last token of every sequence has 383.
All inputs are finite; a program needn't handle non-finite values.
Results may differ from a plain program's by a relative error of at most 0.018.
Values may be sent and summed in bfloat16 or wider, within the bound.
A program may use at most 64 MiB of HBM per device.

v0:
```python
import functools
import math

import jax
import jax.numpy as jnp
from jax import lax
from jax.experimental import pallas as pl
from jax.experimental.pallas import tpu as pltpu
from jax.sharding import PartitionSpec as P

HEAD_DIM = 128
epsilon = 1e-06
masked_score = -1e30
MESH = pl.DeviceIdType.MESH


def flip(index, bit):
    return index + bit - 2 * bit * lax.rem(lax.div(index, bit), 2)


def kernel(
    n, frames_n, x_tile, o_tile,
    tok, gain, wq_hbm, wo_hbm, keys, values, pos, pad,
    out,
    wq, wo, kg, vg, pos_col, raw, xg, qacc, qall, abuf, pbuf, rbuf, sums,
    q_sem, o_sem, own_sem, kv_own, k_send, k_recv, v_send, v_recv,
    x_send, x_recv, p_send, p_recv,
):
    me_f = lax.axis_index("frame")
    me = lax.axis_index("tensor")
    rows = tok.shape[0]
    width = tok.shape[1]
    cols = wq.shape[1]
    span = keys.shape[0]
    bits = [1 << b for b in range(int(math.log2(frames_n)))][::-1]
    phase_n = len(bits)
    v_order = bits[1::-1] + bits[2:] if phase_n > 1 else bits
    n_x = width // x_tile
    n_out = width // o_tile
    lag = n_out // 2
    passed = 0
    has_left = me > 0
    has_right = me < n - 1
    middle = jnp.logical_and(has_left, has_right)
    low_half = 2 * me < n

    def q_load(part):
        window = pl.ds(pl.multiple_of(part * x_tile, x_tile), x_tile)
        return pltpu.make_async_copy(wq_hbm.at[window], wq.at[window], q_sem.at[part])

    def o_load(part):
        depth = cols // 2
        window = pl.ds(part * depth, depth)
        return pltpu.make_async_copy(wo_hbm.at[window], wo.at[window], o_sem.at[part])

    own_x = pltpu.make_async_copy(tok, raw, own_sem)
    own_k = pltpu.make_async_copy(keys, kg.at[pl.ds(0, span)], kv_own.at[0])
    own_v = pltpu.make_async_copy(values, vg.at[pl.ds(0, span)], kv_own.at[1])

    own_x.start()
    barrier = pltpu.get_barrier_semaphore()
    for bit in bits:
        pl.semaphore_signal(
            barrier, inc=1, device_id={"frame": flip(me_f, bit)}, device_id_type=MESH
        )

    @pl.when(has_left)
    def _():
        pl.semaphore_signal(barrier, inc=1, device_id={"tensor": me - 1}, device_id_type=MESH)

    @pl.when(has_right)
    def _():
        pl.semaphore_signal(barrier, inc=1, device_id={"tensor": me + 1}, device_id_type=MESH)

    @pl.when(jnp.logical_not(middle))
    def _():
        pl.semaphore_signal(
            barrier, inc=1, device_id={"tensor": n - 1 - me}, device_id_type=MESH
        )

    own_k.start()
    own_v.start()
    for part in range(n_x):
        q_load(part).start()
    for part in range(2):
        o_load(part).start()

    pos_col[...] = jnp.broadcast_to(pos[...], (HEAD_DIM, n * rows)).T
    own_x.wait()
    hidden = raw[...].astype(jnp.float32)
    factor = lax.rsqrt(jnp.mean(hidden * hidden, axis=-1, keepdims=True) + epsilon)
    xg[me] = (hidden * factor * gain[...]).astype(jnp.bfloat16)

    pl.semaphore_wait(barrier, phase_n + 2)

    def token_copy(block, side, chunk):
        towards = lax.rem(me + 1 - 2 * side + n, n)
        window = pl.ds(pl.multiple_of(chunk * x_tile, x_tile), x_tile)
        return pltpu.make_async_remote_copy(
            src_ref=xg.at[block, :, window],
            dst_ref=xg.at[block, :, window],
            send_sem=x_send.at[side, block, chunk],
            recv_sem=x_recv.at[block, chunk],
            device_id={"tensor": towards},
            device_id_type=MESH,
        )

    for chunk in range(n_x):
        @pl.when(has_right)
        def _():
            token_copy(me, 0, chunk).start()

        @pl.when(has_left)
        def _():
            token_copy(me, 1, chunk).start()

    def exchange(ref, source, send, recv, order, phase):
        bit = order[phase]
        held = [0]
        for earlier in order[:phase]:
            held = held + [slot + earlier for slot in held]
        copies = []
        for slot in held:
            src = source if slot == 0 else ref.at[pl.ds(slot * span, span)]
            copies.append(
                pltpu.make_async_remote_copy(
                    src_ref=src,
                    dst_ref=ref.at[pl.ds((slot + bit) * span, span)],
                    send_sem=send.at[slot + bit],
                    recv_sem=recv.at[slot + bit],
                    device_id={"frame": flip(me_f, bit)},
                    device_id_type=MESH,
                )
            )
        return copies

    phases = [
        exchange(kg, keys, k_send, k_recv, bits, p)
        + exchange(vg, values, v_send, v_recv, v_order, p)
        for p in range(phase_n)
    ]

    def begin(p):
        for copy in phases[p]:
            copy.start()

    def finish(p):
        for copy in phases[p]:
            copy.wait_recv()

    begin(0)

    slot_of = lax.broadcasted_iota(jnp.int32, (1, span), 1)
    pieces = []
    for slot in range(frames_n):
        owner = me_f
        for bit in bits:
            if slot & bit:
                owner = flip(owner, bit)
        pieces.append(slot_of + owner * span)
    frame_index = jnp.concatenate(pieces, axis=1)
    visible_frames = frame_index < frames_n * span - pad[0]

    def q_step(block, side, chunk):
        window = pl.ds(pl.multiple_of(chunk * x_tile, x_tile), x_tile)
        product = jnp.dot(xg[block, :, window], wq[window, :], preferred_element_type=jnp.float32)

        @pl.when(chunk == 0)
        def _():
            qacc[side] = product

        @pl.when(chunk > 0)
        def _():
            qacc[side] += product

        @pl.when(chunk == n_x - 1)
        def _():
            qall[block] = (qacc[side] * HEAD_DIM ** (-0.5)).astype(jnp.bfloat16)

    def own_body(chunk, _):
        q_load(chunk).wait()
        q_step(me, 0, chunk)
        return 0

    lax.fori_loop(0, n_x, own_body, 0)
    for p in range(1, phase_n - 1):
        finish(p - 1)
        begin(p)

    def part_copy(block, side, tile, far=False):
        towards = jnp.where(far, block, lax.rem(me + 1 - 2 * side + n, n))
        slot = jnp.where(far, 1 - side, side)
        window = pl.ds(pl.multiple_of(tile * o_tile, o_tile), o_tile)
        return pltpu.make_async_remote_copy(
            src_ref=pbuf.at[block, :, window],
            dst_ref=rbuf.at[slot, block, :, window],
            send_sem=p_send.at[block, tile],
            recv_sem=p_recv.at[slot, block, tile],
            device_id={"tensor": towards},
            device_id_type=MESH,
        )

    def send_part(block, side, tile, far):
        early = tile < passed
        held = jnp.logical_and(middle, early)

        @pl.when(jnp.logical_not(held))
        def _():
            part_copy(block, side, tile, jnp.logical_and(far, jnp.logical_not(early))).start()

    def attend(block, send, side, far):
        block_pos = pos_col[pl.ds(pl.multiple_of(block * rows, rows), rows), :1]
        visible = (frame_index <= block_pos) & visible_frames
        windows = [slice(i, i + HEAD_DIM) for i in range(0, cols, HEAD_DIM)]
        scores = [
            lax.dot_general(
                qall[block, :, window], kg[:, window], (((1,), (1,)), ((), ())),
                preferred_element_type=jnp.float32,
            )
            for window in windows
        ]
        scores = [jnp.where(visible, score, masked_score) for score in scores]
        highest = [jnp.max(score, axis=-1, keepdims=True) for score in scores]
        weights = [
            jnp.where(visible, jnp.exp(score - top), 0.0) for score, top in zip(scores, highest)
        ]
        totals = [jnp.sum(weight, axis=-1, keepdims=True) for weight in weights]
        gathered = [
            jnp.dot(weight.astype(jnp.bfloat16), vg[:, window], preferred_element_type=jnp.float32)
            for weight, window in zip(weights, windows)
        ]
        for window, value, total in zip(windows, gathered, totals):
            abuf[:, window] = (value / total).astype(jnp.bfloat16)

        def o_body(tile, _):
            window = pl.ds(pl.multiple_of(tile * o_tile, o_tile), o_tile)
            pbuf[block, :, window] = jnp.dot(
                abuf[...], wo[:, window], preferred_element_type=jnp.float32
            ).astype(jnp.bfloat16)
            @pl.when(jnp.logical_and(send, tile > 0))
            def _():
                send_part(block, side, tile - 1, far)

            return 0

        lax.fori_loop(0, n_out, o_body, 0)
        @pl.when(send)
        def _():
            send_part(block, side, n_out - 1, far)

    def stage_body(stage, _):
        before = me - stage
        after = me + stage

        def chunk_body(chunk, _):
            @pl.when(before >= 0)
            def _():
                token_copy(before, 0, chunk).wait_recv()

                @pl.when(has_right)
                def _():
                    token_copy(before, 0, chunk).start()

            @pl.when(after < n)
            def _():
                token_copy(after, 1, chunk).wait_recv()

                @pl.when(has_left)
                def _():
                    token_copy(after, 1, chunk).start()

            def side_body(side, _):
                block = me + (2 * side - 1) * stage

                @pl.when(jnp.logical_and(block >= 0, block < n))
                def _():
                    q_step(block, side, chunk)

                return 0

            lax.fori_loop(0, 2, side_body, 0)
            return 0

        lax.fori_loop(0, n_x, chunk_body, 0)

        @pl.when(stage == 1)
        def _():
            if phase_n > 1:
                finish(phase_n - 2)
                begin(phase_n - 1)
            finish(phase_n - 1)
            own_k.wait()
            own_v.wait()
            for part in range(2):
                o_load(part).wait()

        @pl.when(jnp.logical_or(jnp.logical_not(middle), stage == 1))
        def _():
            end_block = jnp.where(has_left, n - 1 - stage, stage)
            near_block = jnp.where(low_half, me + 1, me - 1)
            block = jnp.where(middle, near_block, end_block)
            ends = jnp.logical_not(middle)
            send = jnp.logical_or(ends, starts_sum(block))
            far = jnp.logical_and(ends, stage == n - 1)
            attend(block, send, jnp.where(block > me, 0, 1), far)

        return 0

    def starts_sum(block):
        up = jnp.logical_and(me == 1, block == n - 1)
        down = jnp.logical_and(me == n - 2, block == 0)
        return jnp.logical_or(up, down)

    lax.fori_loop(1, n, stage_body, 0)

    def relay_body(index, _):
        def side_body(turn, _):
            side = jnp.where(low_half, turn, 1 - turn)
            at = index - turn * lag
            known = jnp.logical_and(at >= 0, at < n * n_out)
            at = jnp.maximum(at, 0)
            stage = lax.div(at, n_out)
            tile = lax.rem(at, n_out)
            known = jnp.logical_and(known, jnp.logical_or(stage > 0, tile >= passed))
            known = jnp.logical_and(known, jnp.logical_or(stage < n - 1, tile < passed))
            stage = jnp.where(stage == 0, n - 1, stage)
            window = pl.ds(pl.multiple_of(tile * o_tile, o_tile), o_tile)
            block = jnp.where(side == 0, stage, n - 1 - stage)
            passes = jnp.where(side == 0, block > me, block < me)
            sent = jnp.logical_and(starts_sum(block), tile >= passed)
            passes = jnp.logical_and(passes, jnp.logical_not(sent))

            @pl.when(jnp.logical_and(known, passes))
            def _():
                part_copy(block, side, tile).wait_recv()
                pbuf[block, :, window] = (
                    pbuf[block, :, window].astype(jnp.float32)
                    + rbuf[side, block, :, window].astype(jnp.float32)
                ).astype(jnp.bfloat16)
                part_copy(block, side, tile).start()

            return 0

        lax.fori_loop(0, 2, side_body, 0)
        return 0

    def late_body(index, _):
        step = jnp.where(low_half, index, n - index)
        block = lax.rem(me + step, n)

        @pl.when(jnp.logical_and(middle, index == n))
        def _():
            lax.fori_loop(0, n * n_out + lag, relay_body, 0)

        @pl.when(jnp.logical_or(middle, index == n))
        def _():
            send = jnp.logical_and(middle, starts_sum(block))
            attend(block, send, jnp.where(block > me, 0, 1), False)

        return 0

    lax.fori_loop(2, n + 1, late_body, 0)

    def sum_body(tile, _):
        window = pl.ds(pl.multiple_of(tile * o_tile, o_tile), o_tile)

        sums[...] = pbuf[me, :, window].astype(jnp.float32)
        for side in range(2):
            from_far = jnp.logical_not(has_right if side else has_left)
            comes = jnp.logical_not(jnp.logical_and(from_far, tile < passed))

            @pl.when(comes)
            def _():
                part_copy(me, side, tile).wait_recv()
                sums[...] += rbuf[side, me, :, window].astype(jnp.float32)

        out[:, window] = sums[...].astype(jnp.bfloat16)
        return 0

    lax.fori_loop(0, n_out, sum_body, 0)

    def drain_body(block, _):
        for tile in range(n_out):
            @pl.when(block != me)
            def _():
                part_copy(block, 0, tile).wait_send()

        for chunk in range(n_x):
            @pl.when(jnp.logical_and(has_right, block <= me))
            def _():
                token_copy(block, 0, chunk).wait_send()

            @pl.when(jnp.logical_and(has_left, block >= me))
            def _():
                token_copy(block, 1, chunk).wait_send()

        return 0

    lax.fori_loop(0, n, drain_body, 0)
    for group in phases:
        for copy in group:
            copy.wait_send()


def divisor(total, most):
    return math.gcd(total, most)


def per_device(
    n, frames_n,
    tokens, norm_gain, query_weight, out_weight, cache_keys, cache_values, token_pos, frame_pad
):
    rows, seqs, width = tokens.shape
    cols = query_weight.shape[1]
    span = cache_keys.shape[0]
    x_tile = divisor(width, 1024)
    o_tile = divisor(width, 1024)
    n_x = width // x_tile
    n_out = width // o_tile
    hbm = pl.BlockSpec(memory_space=pl.ANY)
    vmem = pl.BlockSpec(memory_space=pltpu.VMEM)
    bf16 = jnp.bfloat16
    dma = pltpu.SemaphoreType.DMA
    result = pl.pallas_call(
        functools.partial(kernel, n, frames_n, x_tile, o_tile),
        out_shape=jax.ShapeDtypeStruct((rows, width), bf16),
        in_specs=[hbm, vmem, hbm, hbm, hbm, hbm, vmem, pl.BlockSpec(memory_space=pltpu.SMEM)],
        out_specs=vmem,
        scratch_shapes=[
            pltpu.VMEM(query_weight.shape, bf16),
            pltpu.VMEM(out_weight.shape, bf16),
            pltpu.VMEM((frames_n * span, cols), bf16),
            pltpu.VMEM((frames_n * span, cols), bf16),
            pltpu.VMEM((n * rows, HEAD_DIM), jnp.int32),
            pltpu.VMEM((rows, width), bf16),
            pltpu.VMEM((n, rows, width), bf16),
            pltpu.VMEM((2, rows, cols), jnp.float32),
            pltpu.VMEM((n, rows, cols), bf16),
            pltpu.VMEM((rows, cols), bf16),
            pltpu.VMEM((n, rows, width), bf16),
            pltpu.VMEM((2, n, rows, width), bf16),
            pltpu.VMEM((rows, o_tile), jnp.float32),
            dma((n_x,)),
            dma((2,)),
            dma(()),
            dma((2,)),
            dma((frames_n,)),
            dma((frames_n,)),
            dma((frames_n,)),
            dma((frames_n,)),
            dma((2, n, n_x)),
            dma((n, n_x)),
            dma((n, n_out)),
            dma((2, n, n_out)),
        ],
        compiler_params=pltpu.CompilerParams(collective_id=0, has_side_effects=True),
    )(
        tokens.reshape(rows, width),
        norm_gain.reshape(1, width),
        query_weight,
        out_weight,
        cache_keys.reshape(span, cols),
        cache_values.reshape(span, cols),
        token_pos.reshape(1, n * rows),
        frame_pad,
    )
    return result.reshape(rows, seqs, width)


def solution(mesh):
    placed = (
        P(("frame", "tensor"), None, None),
        P(),
        P(None, "tensor"),
        P("tensor", None),
        P("frame", None, "tensor"),
        P("frame", None, "tensor"),
        P("frame", None),
        P(),
    )
    return jax.shard_map(
        functools.partial(per_device, mesh.shape["tensor"], mesh.shape["frame"]),
        mesh=mesh,
        in_specs=placed,
        out_specs=P(("frame", "tensor"), None, None),
        check_vma=False,
    )
```

profile of v0, /device:TPU:11, one launch (start us, length us, event | category | flops | bytes accessed | tf_op | source)
XLA Modules:
  0.0 46.3 jit_solution(10006673152968413801)
XLA Ops:
  0.7 44.0 %shard_map.82 = bf16[32,4096]{1,0:T(8,128)(2,1)} custom-call(bf16[32,4096]{1,0:T(8,128)(2,1)} %bitcast.7, f32[1,4096]{1,0:T(1,128)} %bitcast.10, bf16[4096,1024]{1,0:T(8,128)(2,1)} %wq_hbm.1, bf16[1024,4096]{1,0:T(8,128)(2,1)} %wo_hbm.1, bf16[48,1024]{1,0:T(8,128)(2,1)} %bitcast.8, bf16[48,1024]{1,0:T(8,128)(2,1)} %bitcast.9, s32[1,128]{1,0:T(1,128)} %bitcast.11, ...), custom_call_target="tpu_custom_call" | custom-call | tf_op jit(solution)/shard_map/pallas_call | solution.py:424
  44.6 1.7 %copy.11 = bf16[32,1,4096]{2,0,1:T(8,128)(2,1)} copy(bf16[32,1,4096]{2,0,1:T(8,128)(2,1)} %bitcast.6) | data formatting | bytes 524288
where the time goes:
time: 46.5 us; the launch traced here: 46.3 us
  Pallas kernels  44 us (95%)
  local copies, waits for them, and re-layouts  1.67 us (4%)
  between operations  0.66 us (1%)
    pallas_call x1, Pallas kernels, per_device(): pl.pallas_call(functools.partial(kernel, n, frames_n, x_tile, o_tile), ou...  44 us
    unnamed x1, local copies, waits for them, and re-layouts  1.67 us

commit v1 on v0

--- a/solution.py
+++ b/solution.py
@@ -20,10 +20,10 @@
 
 def kernel(
     n, frames_n, x_tile, o_tile,
-    tok, gain, wq_hbm, wo_hbm, keys, values, pos, pad,
+    tok, gain_hbm, wq_hbm, wo_hbm, keys, values, pos_hbm, pad,
     out,
-    wq, wo, kg, vg, pos_col, raw, xg, qacc, qall, abuf, pbuf, rbuf, sums,
-    q_sem, o_sem, own_sem, kv_own, k_send, k_recv, v_send, v_recv,
+    wq, wo, kg, vg, pos_col, gain, pos, raw, xg, qacc, qall, abuf, pbuf, rbuf, sums,
+    q_sem, o_sem, own_sem, small_sem, kv_own, k_send, k_recv, v_send, v_recv,
     x_send, x_recv, p_send, p_recv,
 ):
     me_f = lax.axis_index("frame")
@@ -58,6 +58,10 @@
     own_v = pltpu.make_async_copy(values, vg.at[pl.ds(0, span)], kv_own.at[1])
 
     own_x.start()
+    own_gain = pltpu.make_async_copy(gain_hbm, gain, small_sem.at[0])
+    own_pos = pltpu.make_async_copy(pos_hbm, pos, small_sem.at[1])
+    own_gain.start()
+    own_pos.start()
     barrier = pltpu.get_barrier_semaphore()
     for bit in bits:
         pl.semaphore_signal(
@@ -85,8 +89,10 @@
     for part in range(2):
         o_load(part).start()
 
+    own_pos.wait()
     pos_col[...] = jnp.broadcast_to(pos[...], (HEAD_DIM, n * rows)).T
     own_x.wait()
+    own_gain.wait()
     hidden = raw[...].astype(jnp.float32)
     factor = lax.rsqrt(jnp.mean(hidden * hidden, axis=-1, keepdims=True) + epsilon)
     xg[me] = (hidden * factor * gain[...]).astype(jnp.bfloat16)
@@ -417,14 +423,14 @@
     o_tile = divisor(width, 1024)
     n_x = width // x_tile
     n_out = width // o_tile
-    hbm = pl.BlockSpec(memory_space=pl.ANY)
+    hbm = pl.BlockSpec(memory_space=pltpu.HBM)
     vmem = pl.BlockSpec(memory_space=pltpu.VMEM)
     bf16 = jnp.bfloat16
     dma = pltpu.SemaphoreType.DMA
     result = pl.pallas_call(
         functools.partial(kernel, n, frames_n, x_tile, o_tile),
-        out_shape=jax.ShapeDtypeStruct((rows, width), bf16),
-        in_specs=[hbm, vmem, hbm, hbm, hbm, hbm, vmem, pl.BlockSpec(memory_space=pltpu.SMEM)],
+        out_shape=pltpu.VMEM((rows, width), bf16),
+        in_specs=[hbm, hbm, hbm, hbm, hbm, hbm, hbm, pl.BlockSpec(memory_space=pltpu.SMEM)],
         out_specs=vmem,
         scratch_shapes=[
             pltpu.VMEM(query_weight.shape, bf16),
@@ -432,6 +438,8 @@
             pltpu.VMEM((frames_n * span, cols), bf16),
             pltpu.VMEM((frames_n * span, cols), bf16),
             pltpu.VMEM((n * rows, HEAD_DIM), jnp.int32),
+            pltpu.VMEM((1, width), jnp.float32),
+            pltpu.VMEM((1, n * rows), jnp.int32),
             pltpu.VMEM((rows, width), bf16),
             pltpu.VMEM((n, rows, width), bf16),
             pltpu.VMEM((2, rows, cols), jnp.float32),
@@ -443,6 +451,7 @@
             dma((n_x,)),
             dma((2,)),
             dma(()),
+            dma((2,)),
             dma((2,)),
             dma((frames_n,)),
             dma((frames_n,)),

time: 46.5 us -> 44.1 us (0.948)
  Pallas kernels: 44 us -> 42.6 us
  local copies, waits for them, and re-layouts: 1.67 us -> 0.71 us
    pallas_call x1, Pallas kernels: 44 us -> 42.6 us  [per_device(): pl.pallas_call(functools.partial(kernel, n, frames_n, x_tile, o_tile), ou...]
    unnamed x1, local copies, waits for them, and re-layouts: 1.67 us -> 0.71 us
where the time goes in v1:
time: 44.1 us; the launch traced here: 44 us
  Pallas kernels  42.6 us (97%)
  local copies, waits for them, and re-layouts  0.71 us (2%)
  between operations  0.66 us (1%)
    pallas_call x1, Pallas kernels, per_device(): pl.pallas_call(functools.partial(kernel, n, frames_n, x_tile, o_tile), ou...  42.6 us

profile of v1, /device:TPU:11, one launch (start us, length us, event | category | flops | bytes accessed | tf_op | source)
XLA Modules:
  0.0 44.0 jit_solution(7072700031406662119)
XLA Ops:
  0.7 42.6 %shard_map.82 = bf16[32,4096]{1,0:T(8,128)(2,1)S(1)} custom-call(bf16[32,4096]{1,0:T(8,128)(2,1)} %bitcast.7, f32[1,4096]{1,0:T(1,128)} %bitcast.10, bf16[4096,1024]{1,0:T(8,128)(2,1)} %wq_hbm.1, bf16[1024,4096]{1,0:T(8,128)(2,1)} %wo_hbm.1, bf16[48,1024]{1,0:T(8,128)(2,1)} %bitcast.8, bf16[48,1024]{1,0:T(8,128)(2,1)} %bitcast.9, s32[1,128]{1,0:T(1,128)} %bitcast.11, ...), custom_call_target="tpu_custom_call" | custom-call | tf_op jit(solution)/shard_map/pallas_call | solution.py:430
  43.3 0.7 %copy.10 = bf16[32,1,4096]{2,0,1:T(8,128)(2,1)} copy(bf16[32,1,4096]{2,0,1:T(8,128)(2,1)S(1)} %bitcast.6) | data formatting | bytes 524288

commit v2 on v1

v2 whole, which is shorter than its diff:
```python
import functools
import math

import jax
import jax.numpy as jnp
from jax import lax
from jax.experimental import pallas as pl
from jax.experimental.pallas import tpu as pltpu
from jax.sharding import PartitionSpec as P

HEAD_DIM = 128
epsilon = 1e-06
masked_score = -1e30
MESH = pl.DeviceIdType.MESH


def flip(index, bit):
    return index + bit - 2 * bit * lax.rem(lax.div(index, bit), 2)


def kernel(
    n, frames_n, x_tile, o_tile, p_tile, lag, direct, early,
    tok, gain_hbm, wq_hbm, wo_hbm, keys, values, pos_hbm, pad,
    out,
    wq, wo, kg, vg, pos_col, gain, pos, raw, xg, qacc, qall, abuf, pbuf, rbuf,
    q_sem, o_sem, own_sem, small_sem, kv_own, k_send, k_recv, v_send, v_recv,
    x_send, x_recv, p_send, p_recv,
):
    me_f = lax.axis_index("frame")
    me = lax.axis_index("tensor")
    rows = tok.shape[0]
    width = tok.shape[1]
    cols = wq.shape[1]
    span = keys.shape[0]
    bits = [1 << b for b in range(int(math.log2(frames_n)))][::-1]
    phase_n = len(bits)
    k_order = bits
    v_order = bits[1::-1] + bits[2:] if phase_n > 1 else bits
    n_x = width // x_tile
    n_out = width // o_tile
    n_part = width // p_tile
    per_out = o_tile // p_tile
    chained = n_part - direct
    has_left = me > 0
    has_right = me < n - 1
    middle = jnp.logical_and(has_left, has_right)
    low_half = 2 * me < n

    def q_load(part):
        window = pl.ds(part * x_tile, x_tile)
        return pltpu.make_async_copy(wq_hbm.at[window], wq.at[window], q_sem.at[part])

    def o_load(part):
        depth = cols // 2
        window = pl.ds(part * depth, depth)
        return pltpu.make_async_copy(wo_hbm.at[window], wo.at[window], o_sem.at[part])

    def rows_of(block, count=1):
        return pl.ds(pl.multiple_of(block * rows, rows), count * rows)

    own_x = pltpu.make_async_copy(tok, raw, own_sem)
    own_gain = pltpu.make_async_copy(gain_hbm, gain, small_sem.at[0])
    own_pos = pltpu.make_async_copy(pos_hbm, pos, small_sem.at[1])
    own_k = pltpu.make_async_copy(keys, kg.at[pl.ds(0, span)], kv_own.at[0])
    own_v = pltpu.make_async_copy(values, vg.at[pl.ds(0, span)], kv_own.at[1])

    barrier = pltpu.get_barrier_semaphore()
    for bit in bits:
        pl.semaphore_signal(
            barrier, inc=1, device_id={"frame": flip(me_f, bit)}, device_id_type=MESH
        )

    @pl.when(has_left)
    def _():
        pl.semaphore_signal(barrier, inc=1, device_id={"tensor": me - 1}, device_id_type=MESH)

    @pl.when(has_right)
    def _():
        pl.semaphore_signal(barrier, inc=1, device_id={"tensor": me + 1}, device_id_type=MESH)

    own_x.start()
    own_gain.start()
    own_pos.start()
    own_k.start()
    own_v.start()

    own_x.wait()
    own_gain.wait()
    own_k.wait()
    own_v.wait()
    for part in range(n_x):
        q_load(part).start()
    for part in range(2):
        o_load(part).start()
    hidden = raw[...].astype(jnp.float32)
    factor = lax.rsqrt(jnp.mean(hidden * hidden, axis=-1, keepdims=True) + epsilon)
    xg[rows_of(me), :] = (hidden * factor * gain[...]).astype(jnp.bfloat16)
    own_pos.wait()
    pos_col[...] = jnp.broadcast_to(pos[...], (HEAD_DIM, n * rows)).T

    pl.semaphore_wait(
        barrier, phase_n + has_left.astype(jnp.int32) + has_right.astype(jnp.int32)
    )

    def neighbour(side):
        return lax.rem(me + 1 - 2 * side + n, n)

    def token_copy(block, side, chunk):
        window = pl.ds(chunk * x_tile, x_tile)
        if not isinstance(chunk, int):
            window = pl.ds(pl.multiple_of(chunk * x_tile, x_tile), x_tile)
        return pltpu.make_async_remote_copy(
            src_ref=xg.at[rows_of(block), window],
            dst_ref=xg.at[rows_of(block), window],
            send_sem=x_send.at[side, block, chunk],
            recv_sem=x_recv.at[block, chunk],
            device_id={"tensor": neighbour(side)},
            device_id_type=MESH,
        )

    for chunk in range(n_x):
        @pl.when(has_right)
        def _():
            token_copy(me, 0, chunk).start()

        @pl.when(has_left)
        def _():
            token_copy(me, 1, chunk).start()

    def frame_copy(ref, slot, bit, send, recv):
        return pltpu.make_async_remote_copy(
            src_ref=ref.at[pl.ds(slot * span, span)],
            dst_ref=ref.at[pl.ds((slot + bit) * span, span)],
            send_sem=send.at[slot + bit],
            recv_sem=recv.at[slot + bit],
            device_id={"frame": flip(me_f, bit)},
            device_id_type=MESH,
        )

    def plan(ref, order, send, recv):
        steps, held = [], [0]
        for p, bit in enumerate(order):
            fresh = [slot + bit for slot in held]
            for slot in fresh:
                arrival = frame_copy(ref, slot - bit, bit, send, recv)
                onward = [frame_copy(ref, slot, later, send, recv) for later in order[p + 1:]]
                steps.append((arrival, onward))
            held = held + fresh
        own = [frame_copy(ref, 0, bit, send, recv) for bit in order]
        return own, steps

    k_own, k_steps = plan(kg, k_order, k_send, k_recv)
    v_own, v_steps = plan(vg, v_order, v_send, v_recv)
    for pair in zip(k_own, v_own):
        for copy in pair:
            copy.start()
    relays = [pair for pair in zip(k_steps, v_steps) if pair[0][1]]
    last_ones = [pair for pair in zip(k_steps, v_steps) if not pair[0][1]]

    def frame_step(pair):
        for arrival, onward in pair:
            arrival.wait_recv()
            for copy in onward:
                copy.start()

    def frame_steps(chunk):
        if chunk < n_x - 2:
            for pair in relays[chunk:chunk + 1]:
                frame_step(pair)
        if chunk == n_x - 1:
            for pair in relays[max(n_x - 2, 0):]:
                frame_step(pair)

    def frames_done():
        for pair in last_ones:
            frame_step(pair)

    slot_of = lax.broadcasted_iota(jnp.int32, (1, span), 1)
    pieces = []
    for slot in range(frames_n):
        owner = me_f
        for bit in bits:
            if slot & bit:
                owner = flip(owner, bit)
        pieces.append(slot_of + owner * span)
    frame_index = jnp.concatenate(pieces, axis=1)
    visible_frames = frame_index < frames_n * span - pad[0]

    scale = HEAD_DIM ** (-0.5)

    def q_first(block, count, chunk):
        window = slice(chunk * x_tile, (chunk + 1) * x_tile)
        at = rows_of(block, count)
        held = pl.ds(0, count * rows)
        product = jnp.dot(xg[at, window], wq[window, :], preferred_element_type=jnp.float32)
        if chunk > 0:
            product = qacc[held, :] + product
        if chunk < n_x - 1:
            qacc[held, :] = product
        else:
            qall[at, :] = (product * scale).astype(jnp.bfloat16)

    def q_step(block, place, chunk):
        window = pl.ds(pl.multiple_of(chunk * x_tile, x_tile), x_tile)
        held = pl.ds(place * rows, rows)
        if not isinstance(place, int):
            held = rows_of(place)
        product = jnp.dot(
            xg[rows_of(block), window], wq[window, :], preferred_element_type=jnp.float32
        )

        @pl.when(chunk == 0)
        def _():
            qacc[held, :] = product

        @pl.when(chunk > 0)
        def _():
            qacc[held, :] += product

        @pl.when(chunk == n_x - 1)
        def _():
            qall[rows_of(block), :] = (qacc[held, :] * scale).astype(jnp.bfloat16)

    def attend(block, count):
        at = rows_of(block, count)
        visible = (frame_index <= pos_col[at, :1]) & visible_frames
        windows = [slice(i, i + HEAD_DIM) for i in range(0, cols, HEAD_DIM)]
        scores = [
            lax.dot_general(
                qall[at, window], kg[:, window], (((1,), (1,)), ((), ())),
                preferred_element_type=jnp.float32,
            )
            for window in windows
        ]
        scores = [jnp.where(visible, score, masked_score) for score in scores]
        highest = [jnp.max(score, axis=-1, keepdims=True) for score in scores]
        weights = [
            jnp.where(visible, jnp.exp(score - top), 0.0) for score, top in zip(scores, highest)
        ]
        totals = [jnp.sum(weight, axis=-1, keepdims=True) for weight in weights]
        gathered = [
            jnp.dot(weight.astype(jnp.bfloat16), vg[:, window], preferred_element_type=jnp.float32)
            for weight, window in zip(weights, windows)
        ]
        for window, value, total in zip(windows, gathered, totals):
            abuf[at, window] = (value / total).astype(jnp.bfloat16)

    def part_window(tile):
        return pl.ds(pl.multiple_of(tile * p_tile, p_tile), p_tile)

    def part_copy(block, side, tile, far=False):
        slot = jnp.where(far, 1 - side, side)
        towards = jnp.where(far, block, neighbour(side))
        return pltpu.make_async_remote_copy(
            src_ref=pbuf.at[rows_of(block), part_window(tile)],
            dst_ref=rbuf.at[slot, rows_of(block), part_window(tile)],
            send_sem=p_send.at[block, tile],
            recv_sem=p_recv.at[slot, block, tile],
            device_id={"tensor": towards},
            device_id_type=MESH,
        )

    def project(block, count, first_tile, send):
        at = rows_of(block, count)

        def body(index, _):
            tile = lax.rem(index + first_tile, n_out)
            window = pl.ds(pl.multiple_of(tile * o_tile, o_tile), o_tile)
            pbuf[at, window] = jnp.dot(
                abuf[at, :], wo[:, window], preferred_element_type=jnp.float32
            ).astype(jnp.bfloat16)

            @pl.when(index > 0)
            def _():
                send(lax.rem(tile + n_out - 1, n_out))

            return 0

        lax.fori_loop(0, n_out, body, 0)
        send((first_tile + n_out - 1) % n_out)

    def parts_of(tile):
        return [tile * per_out + part for part in range(per_out)]

    def drain_inputs():
        def drain_body(block, _):
            for chunk in range(n_x):
                @pl.when(jnp.logical_and(has_right, block <= me))
                def _():
                    token_copy(block, 0, chunk).wait_send()

                @pl.when(jnp.logical_and(has_left, block >= me))
                def _():
                    token_copy(block, 1, chunk).wait_send()

            return 0

        lax.fori_loop(0, n, drain_body, 0)
        for own, steps in ((k_own, k_steps), (v_own, v_steps)):
            for copy in own:
                copy.wait_send()
            for _, onward in steps:
                for copy in onward:
                    copy.wait_send()

    @pl.when(jnp.logical_not(middle))
    def _():
        heading = jnp.where(has_left, -1, 1)
        arriving = jnp.where(has_left, 0, 1)
        leaving = 1 - arriving
        near = me + heading
        first = jnp.minimum(me, near)
        for chunk in range(n_x):
            q_load(chunk).wait()
            token_copy(near, arriving, chunk).wait_recv()
            q_first(first, 2, chunk)
            frame_steps(chunk)
        frames_done()
        attend(first, 2)
        for part in range(2):
            o_load(part).wait()


        def send_near(tile):
            for part in parts_of(tile):
                part_copy(near, leaving, part).start()

        project(first, 2, 0, send_near)

        def stage_body(stage, _):
            block = me + heading * stage

            def chunk_body(chunk, _):
                token_copy(block, arriving, chunk).wait_recv()
                q_step(block, 0, chunk)
                return 0

            lax.fori_loop(0, n_x, chunk_body, 0)
            attend(block, 1)

            def send_block(tile):
                for part in parts_of(tile):
                    far = jnp.logical_and(stage == n - 1, part >= chained)
                    part_copy(block, leaving, part, far).start()

            project(block, 1, 0, send_block)
            return 0

        lax.fori_loop(2, n, stage_body, 0)
        drain_inputs()

        def sum_body(tile, _):
            window = part_window(tile)
            part_copy(me, arriving, tile).wait_recv()
            total = pbuf[rows_of(me), window].astype(jnp.float32)
            total = total + rbuf[arriving, rows_of(me), window].astype(jnp.float32)

            @pl.when(tile < chained)
            def _():
                out[:, window] = total.astype(jnp.bfloat16)

            @pl.when(tile >= chained)
            def _():
                part_copy(me, leaving, tile).wait_recv()
                straight = rbuf[leaving, rows_of(me), window].astype(jnp.float32)
                out[:, window] = (total + straight).astype(jnp.bfloat16)

            return 0

        def sum_index(index, _):
            return sum_body(lax.rem(index + chained, n_part), 0)

        lax.fori_loop(0, n_part, sum_index, 0)

    @pl.when(middle)
    def _():
        for chunk in range(n_x):
            q_load(chunk).wait()
            for side, block in ((0, me - 1), (1, me + 1)):
                token_copy(block, side, chunk).wait_recv()
                token_copy(block, side, chunk).start()
            q_first(me - 1, 3, chunk)
            frame_steps(chunk)

        def stage_body(stage, _):
            def chunk_body(chunk, _):
                def side_body(side, _):
                    block = me - stage + 2 * side * stage

                    @pl.when(jnp.logical_and(block >= 0, block < n))
                    def _():
                        token_copy(block, side, chunk).wait_recv()
                        token_copy(block, side, chunk).start()
                        q_step(block, side, chunk)

                    return 0

                lax.fori_loop(0, 2, side_body, 0)
                return 0

            lax.fori_loop(0, n_x, chunk_body, 0)
            return 0

        lax.fori_loop(2, n - 1, stage_body, 0)
        frames_done()
        groups = max(1, n * rows // HEAD_DIM)
        while n % groups:
            groups -= 1
        count = n // groups
        for part in range(2):
            o_load(part).wait()

        def group_body(group, _):
            attend(group * count, count)

            def send_started(tile):
                last = group == groups - 1
                for part in parts_of(tile):
                    @pl.when((me == 1) & last & (part >= chained))
                    def _():
                        part_copy(n - 1, 0, part).start()

                    @pl.when((me == n - 2) & (group == 0) & (part >= chained))
                    def _():
                        part_copy(0, 1, part).start()

            project(group * count, count, chained // per_out % n_out, send_started)
            return 0

        lax.fori_loop(0, groups, group_body, 0)

        def relay(block, side, tile):
            at = rows_of(block)
            window = part_window(tile)
            part_copy(block, side, tile).wait_recv()
            pbuf[at, window] = (
                pbuf[at, window].astype(jnp.float32)
                + rbuf[side, at, window].astype(jnp.float32)
            ).astype(jnp.bfloat16)
            part_copy(block, side, tile).start()

        def relay_body(index, _):
            def side_body(turn, _):
                side = jnp.where(low_half, turn, 1 - turn)
                at = index - turn * lag
                stage = 1 + lax.div(jnp.maximum(at, 0), n_part)
                tile = lax.rem(jnp.maximum(at, 0), n_part)
                block = jnp.where(side == 0, stage, n - 1 - stage)
                passes = jnp.where(side == 0, block > me, block < me)
                chain = (stage < n - 1) | ((stage == n - 1) & (tile < chained))

                @pl.when((at >= 0) & chain & passes)
                def _():
                    relay(block, side, tile)

                far = index - (n - 3) * n_part - early
                beside = jnp.where(side == 0, me == 1, me == n - 2)

                @pl.when((far >= 0) & (far < direct) & jnp.logical_not(beside))
                def _():
                    relay(jnp.where(side == 0, n - 1, 0), side, chained + far)

                return 0

            lax.fori_loop(0, 2, side_body, 0)
            return 0

        behind = jnp.minimum(me, n - 1 - me) * n_part
        lax.fori_loop(jnp.minimum(behind, (n - 3) * n_part), (n - 1) * n_part + lag, relay_body, 0)

        def sum_body(tile, _):
            window = part_window(tile)
            total = pbuf[rows_of(me), window].astype(jnp.float32)
            for side in range(2):
                part_copy(me, side, tile).wait_recv()
                total = total + rbuf[side, rows_of(me), window].astype(jnp.float32)
            out[:, window] = total.astype(jnp.bfloat16)
            return 0

        lax.fori_loop(0, n_part, sum_body, 0)
        drain_inputs()

    def drain_body(block, _):
        @pl.when(block != me)
        def _():
            for tile in range(n_part):
                part_copy(block, 0, tile).wait_send()

        return 0

    lax.fori_loop(0, n, drain_body, 0)


def divisor(total, most):
    return math.gcd(total, most)


def per_device(
    n, frames_n,
    tokens, norm_gain, query_weight, out_weight, cache_keys, cache_values, token_pos, frame_pad
):
    rows, seqs, width = tokens.shape
    cols = query_weight.shape[1]
    span = cache_keys.shape[0]
    x_tile = divisor(width, 1024)
    o_tile = divisor(width, 512)
    p_tile = divisor(o_tile, 256)
    n_x = width // x_tile
    n_part = width // p_tile
    lag = max(1, 5 * n_part // 8)
    direct = n_part if n > 2 else 0
    early = n_part // 4
    hbm = pl.BlockSpec(memory_space=pltpu.HBM)
    vmem = pl.BlockSpec(memory_space=pltpu.VMEM)
    bf16 = jnp.bfloat16
    dma = pltpu.SemaphoreType.DMA
    result = pl.pallas_call(
        functools.partial(kernel, n, frames_n, x_tile, o_tile, p_tile, lag, direct, early),
        out_shape=pltpu.VMEM((rows, width), bf16),
        in_specs=[hbm, hbm, hbm, hbm, hbm, hbm, hbm, pl.BlockSpec(memory_space=pltpu.SMEM)],
        out_specs=vmem,
        scratch_shapes=[
            pltpu.VMEM(query_weight.shape, bf16),
            pltpu.VMEM(out_weight.shape, bf16),
            pltpu.VMEM((frames_n * span, cols), bf16),
            pltpu.VMEM((frames_n * span, cols), bf16),
            pltpu.VMEM((n * rows, HEAD_DIM), jnp.int32),
            pltpu.VMEM((1, width), jnp.float32),
            pltpu.VMEM((1, n * rows), jnp.int32),
            pltpu.VMEM((rows, width), bf16),
            pltpu.VMEM((n * rows, width), bf16),
            pltpu.VMEM((3 * rows, cols), jnp.float32),
            pltpu.VMEM((n * rows, cols), bf16),
            pltpu.VMEM((n * rows, cols), bf16),
            pltpu.VMEM((n * rows, width), bf16),
            pltpu.VMEM((2, n * rows, width), bf16),
            dma((n_x,)),
            dma((2,)),
            dma(()),
            dma((2,)),
            dma((2,)),
            dma((frames_n,)),
            dma((frames_n,)),
            dma((frames_n,)),
            dma((frames_n,)),
            dma((2, n, n_x)),
            dma((n, n_x)),
            dma((n, n_part)),
            dma((2, n, n_part)),
        ],
        compiler_params=pltpu.CompilerParams(collective_id=0, has_side_effects=True),
    )(
        tokens.reshape(rows, width),
        norm_gain.reshape(1, width),
        query_weight,
        out_weight,
        cache_keys.reshape(span, cols),
        cache_values.reshape(span, cols),
        token_pos.reshape(1, n * rows),
        frame_pad,
    )
    return result.reshape(rows, seqs, width)


def solution(mesh):
    placed = (
        P(("frame", "tensor"), None, None),
        P(),
        P(None, "tensor"),
        P("tensor", None),
        P("frame", None, "tensor"),
        P("frame", None, "tensor"),
        P("frame", None),
        P(),
    )
    return jax.shard_map(
        functools.partial(per_device, mesh.shape["tensor"], mesh.shape["frame"]),
        mesh=mesh,
        in_specs=placed,
        out_specs=P(("frame", "tensor"), None, None),
        check_vma=False,
    )
```

time: 44.1 us -> 41.4 us (0.939)
  the two profiles are of different devices: /device:TPU:11 before, /device:TPU:0 now
where the time goes in v2:
time: 41.4 us; the launch traced here: 41.2 us
  Pallas kernels  39.9 us (96%)
  local copies, waits for them, and re-layouts  0.71 us (2%)
  between operations  0.66 us (2%)
    pallas_call x1, Pallas kernels, per_device(): pl.pallas_call(functools.partial(kernel, n, frames_n, x_tile, o_tile, p_t...  39.9 us

profile of v2, /device:TPU:0, one launch (start us, length us, event | category | flops | bytes accessed | tf_op | source)
XLA Modules:
  0.0 41.2 jit_solution(8054761890091815649)
XLA Ops:
  0.7 39.9 %shard_map.82 = bf16[32,4096]{1,0:T(8,128)(2,1)S(1)} custom-call(bf16[32,4096]{1,0:T(8,128)(2,1)} %bitcast.7, f32[1,4096]{1,0:T(1,128)} %bitcast.10, bf16[4096,1024]{1,0:T(8,128)(2,1)} %wq_hbm.1, bf16[1024,4096]{1,0:T(8,128)(2,1)} %wo_hbm.1, bf16[48,1024]{1,0:T(8,128)(2,1)} %bitcast.8, bf16[48,1024]{1,0:T(8,128)(2,1)} %bitcast.9, s32[1,128]{1,0:T(1,128)} %bitcast.11, ...), custom_call_target="tpu_custom_call" | custom-call | tf_op jit(solution)/shard_map/pallas_call | solution.py:517
  40.5 0.7 %copy.10 = bf16[32,1,4096]{2,0,1:T(8,128)(2,1)} copy(bf16[32,1,4096]{2,0,1:T(8,128)(2,1)S(1)} %bitcast.6) | data formatting | bytes 524288

commit v3 on v2

--- a/solution.py
+++ b/solution.py
@@ -112,7 +112,7 @@
         return pltpu.make_async_remote_copy(
             src_ref=xg.at[rows_of(block), window],
             dst_ref=xg.at[rows_of(block), window],
-            send_sem=x_send.at[side, block, chunk],
+            send_sem=x_send.at[side, block],
             recv_sem=x_recv.at[block, chunk],
             device_id={"tensor": neighbour(side)},
             device_id_type=MESH,
@@ -127,35 +127,48 @@
         def _():
             token_copy(me, 1, chunk).start()
 
-    def frame_copy(ref, slot, bit, send, recv):
+    def frame_copy(ref, slot, bit, last, send, recv):
+        target = slot + bit
+        index = 0 if target & last else target % last + target // (2 * last) * last
         return pltpu.make_async_remote_copy(
             src_ref=ref.at[pl.ds(slot * span, span)],
-            dst_ref=ref.at[pl.ds((slot + bit) * span, span)],
-            send_sem=send.at[slot + bit],
-            recv_sem=recv.at[slot + bit],
+            dst_ref=ref.at[pl.ds(target * span, span)],
+            send_sem=send,
+            recv_sem=recv.at[index],
             device_id={"frame": flip(me_f, bit)},
             device_id_type=MESH,
         )
 
     def plan(ref, order, send, recv):
         steps, held = [], [0]
-        for p, bit in enumerate(order):
+        last = order[-1]
+        for p, bit in enumerate(order[:-1]):
             fresh = [slot + bit for slot in held]
             for slot in fresh:
-                arrival = frame_copy(ref, slot - bit, bit, send, recv)
-                onward = [frame_copy(ref, slot, later, send, recv) for later in order[p + 1:]]
+                arrival = frame_copy(ref, slot - bit, bit, last, send, recv)
+                onward = [
+                    frame_copy(ref, slot, later, last, send, recv) for later in order[p + 1:]
+                ]
                 steps.append((arrival, onward))
             held = held + fresh
-        own = [frame_copy(ref, 0, bit, send, recv) for bit in order]
-        return own, steps
-
-    k_own, k_steps = plan(kg, k_order, k_send, k_recv)
-    v_own, v_steps = plan(vg, v_order, v_send, v_recv)
+        own = [frame_copy(ref, 0, bit, last, send, recv) for bit in order]
+        half = pl.ds(0, len(held) * span)
+        rest = pltpu.make_async_remote_copy(
+            src_ref=ref.at[half],
+            dst_ref=ref.at[half],
+            send_sem=send,
+            recv_sem=recv.at[0],
+            device_id={"frame": flip(me_f, last)},
+            device_id_type=MESH,
+        )
+        return own, steps, rest
+
+    k_own, k_steps, k_rest = plan(kg, k_order, k_send, k_recv)
+    v_own, v_steps, v_rest = plan(vg, v_order, v_send, v_recv)
     for pair in zip(k_own, v_own):
         for copy in pair:
             copy.start()
-    relays = [pair for pair in zip(k_steps, v_steps) if pair[0][1]]
-    last_ones = [pair for pair in zip(k_steps, v_steps) if not pair[0][1]]
+    relays = list(zip(k_steps, v_steps))
 
     def frame_step(pair):
         for arrival, onward in pair:
@@ -172,8 +185,8 @@
                 frame_step(pair)
 
     def frames_done():
-        for pair in last_ones:
-            frame_step(pair)
+        k_rest.wait_recv()
+        v_rest.wait_recv()
 
     slot_of = lax.broadcasted_iota(jnp.int32, (1, span), 1)
     pieces = []
@@ -248,17 +261,24 @@
     def part_window(tile):
         return pl.ds(pl.multiple_of(tile * p_tile, p_tile), p_tile)
 
-    def part_copy(block, side, tile, far=False):
+    def part_move(block, side, tile, far, receiver):
         slot = jnp.where(far, 1 - side, side)
         towards = jnp.where(far, block, neighbour(side))
+        receiver = towards if receiver is None else receiver
         return pltpu.make_async_remote_copy(
             src_ref=pbuf.at[rows_of(block), part_window(tile)],
             dst_ref=rbuf.at[slot, rows_of(block), part_window(tile)],
-            send_sem=p_send.at[block, tile],
-            recv_sem=p_recv.at[slot, block, tile],
+            send_sem=p_send,
+            recv_sem=p_recv.at[jnp.where((slot == 1) & (block == receiver), n, block), tile],
             device_id={"tensor": towards},
             device_id_type=MESH,
         )
+
+    def part_copy(block, side, tile, far=False):
+        return part_move(block, side, tile, far, None)
+
+    def part_here(block, side, tile):
+        return part_move(block, side, tile, False, me)
 
     def project(block, count, first_tile, send):
         at = rows_of(block, count)
@@ -284,24 +304,31 @@
 
     def drain_inputs():
         def drain_body(block, _):
-            for chunk in range(n_x):
-                @pl.when(jnp.logical_and(has_right, block <= me))
+            for side, sent in ((0, has_right & (block <= me)), (1, has_left & (block >= me))):
+                @pl.when(sent)
                 def _():
-                    token_copy(block, 0, chunk).wait_send()
-
-                @pl.when(jnp.logical_and(has_left, block >= me))
-                def _():
-                    token_copy(block, 1, chunk).wait_send()
+                    pltpu.make_async_remote_copy(
+                        src_ref=xg.at[rows_of(block)],
+                        dst_ref=xg.at[rows_of(block)],
+                        send_sem=x_send.at[side, block],
+                        recv_sem=x_recv.at[block, 0],
+                        device_id={"tensor": neighbour(side)},
+                        device_id_type=MESH,
+                    ).wait_send()
 
             return 0
 
         lax.fori_loop(0, n, drain_body, 0)
-        for own, steps in ((k_own, k_steps), (v_own, v_steps)):
-            for copy in own:
-                copy.wait_send()
-            for _, onward in steps:
-                for copy in onward:
-                    copy.wait_send()
+        others = pl.ds(0, (frames_n - 1) * span)
+        for ref, send, recv in ((kg, k_send, k_recv), (vg, v_send, v_recv)):
+            pltpu.make_async_remote_copy(
+                src_ref=ref.at[others],
+                dst_ref=ref.at[others],
+                send_sem=send,
+                recv_sem=recv.at[0],
+                device_id={"frame": flip(me_f, bits[0])},
+                device_id_type=MESH,
+            ).wait_send()
 
     @pl.when(jnp.logical_not(middle))
     def _():
@@ -351,7 +378,7 @@
 
         def sum_body(tile, _):
             window = part_window(tile)
-            part_copy(me, arriving, tile).wait_recv()
+            part_here(me, arriving, tile).wait_recv()
             total = pbuf[rows_of(me), window].astype(jnp.float32)
             total = total + rbuf[arriving, rows_of(me), window].astype(jnp.float32)
 
@@ -361,7 +388,7 @@
 
             @pl.when(tile >= chained)
             def _():
-                part_copy(me, leaving, tile).wait_recv()
+                part_here(me, leaving, tile).wait_recv()
                 straight = rbuf[leaving, rows_of(me), window].astype(jnp.float32)
                 out[:, window] = (total + straight).astype(jnp.bfloat16)
 
@@ -432,7 +459,7 @@
         def relay(block, side, tile):
             at = rows_of(block)
             window = part_window(tile)
-            part_copy(block, side, tile).wait_recv()
+            part_here(block, side, tile).wait_recv()
             pbuf[at, window] = (
                 pbuf[at, window].astype(jnp.float32)
                 + rbuf[side, at, window].astype(jnp.float32)
@@ -466,13 +493,13 @@
             return 0
 
         behind = jnp.minimum(me, n - 1 - me) * n_part
-        lax.fori_loop(jnp.minimum(behind, (n - 3) * n_part), (n - 1) * n_part + lag, relay_body, 0)
+        lax.fori_loop(jnp.minimum(behind, (n - 3) * n_part + early), (n - 1) * n_part + lag, relay_body, 0)
 
         def sum_body(tile, _):
             window = part_window(tile)
             total = pbuf[rows_of(me), window].astype(jnp.float32)
             for side in range(2):
-                part_copy(me, side, tile).wait_recv()
+                part_here(me, side, tile).wait_recv()
                 total = total + rbuf[side, rows_of(me), window].astype(jnp.float32)
             out[:, window] = total.astype(jnp.bfloat16)
             return 0
@@ -480,15 +507,15 @@
         lax.fori_loop(0, n_part, sum_body, 0)
         drain_inputs()
 
-    def drain_body(block, _):
-        @pl.when(block != me)
-        def _():
-            for tile in range(n_part):
-                part_copy(block, 0, tile).wait_send()
-
-        return 0
-
-    lax.fori_loop(0, n, drain_body, 0)
+    others = pl.ds(0, (n - 1) * rows)
+    pltpu.make_async_remote_copy(
+        src_ref=pbuf.at[others],
+        dst_ref=rbuf.at[0, others],
+        send_sem=p_send,
+        recv_sem=p_recv.at[0, 0],
+        device_id={"tensor": neighbour(0)},
+        device_id_type=MESH,
+    ).wait_send()
 
 
 def divisor(total, most):
@@ -504,12 +531,12 @@
     span = cache_keys.shape[0]
     x_tile = divisor(width, 1024)
     o_tile = divisor(width, 512)
-    p_tile = divisor(o_tile, 256)
+    p_tile = divisor(o_tile, 512)
     n_x = width // x_tile
     n_part = width // p_tile
     lag = max(1, 5 * n_part // 8)
     direct = n_part if n > 2 else 0
-    early = n_part // 4
+    early = -(3 * n_part // 8)
     hbm = pl.BlockSpec(memory_space=pltpu.HBM)
     vmem = pl.BlockSpec(memory_space=pltpu.VMEM)
     bf16 = jnp.bfloat16
@@ -539,14 +566,14 @@
             dma(()),
             dma((2,)),
             dma((2,)),
-            dma((frames_n,)),
-            dma((frames_n,)),
-            dma((frames_n,)),
-            dma((frames_n,)),
-            dma((2, n, n_x)),
+            dma(()),
+            dma((frames_n // 2,)),
+            dma(()),
+            dma((frames_n // 2,)),
+            dma((2, n)),
             dma((n, n_x)),
-            dma((n, n_part)),
-            dma((2, n, n_part)),
+            dma(()),
+            dma((n + 1, n_part)),
         ],
         compiler_params=pltpu.CompilerParams(collective_id=0, has_side_effects=True),
     )(

time: 41.4 us -> 38 us (0.918)
  the two profiles are of different devices: /device:TPU:0 before, /device:TPU:11 now
where the time goes in v3:
time: 38 us; the launch traced here: 37.6 us
  Pallas kernels  36.2 us (95%)
  local copies, waits for them, and re-layouts  0.71 us (2%)
  between operations  0.66 us (2%)
    pallas_call x1, Pallas kernels, per_device(): pl.pallas_call(functools.partial(kernel, n, frames_n, x_tile, o_tile, p_t...  36.2 us

profile of v3, /device:TPU:11, one launch (start us, length us, event | category | flops | bytes accessed | tf_op | source)
XLA Modules:
  0.0 37.6 jit_solution(402001569822960569)
XLA Ops:
  0.7 36.2 %shard_map.82 = bf16[32,4096]{1,0:T(8,128)(2,1)S(1)} custom-call(bf16[32,4096]{1,0:T(8,128)(2,1)} %bitcast.7, f32[1,4096]{1,0:T(1,128)} %bitcast.10, bf16[4096,1024]{1,0:T(8,128)(2,1)} %wq_hbm.1, bf16[1024,4096]{1,0:T(8,128)(2,1)} %wo_hbm.1, bf16[48,1024]{1,0:T(8,128)(2,1)} %bitcast.8, bf16[48,1024]{1,0:T(8,128)(2,1)} %bitcast.9, s32[1,128]{1,0:T(1,128)} %bitcast.11, ...), custom_call_target="tpu_custom_call" | custom-call | tf_op jit(solution)/shard_map/pallas_call | solution.py:544
  36.9 0.7 %copy.10 = bf16[32,1,4096]{2,0,1:T(8,128)(2,1)} copy(bf16[32,1,4096]{2,0,1:T(8,128)(2,1)S(1)} %bitcast.6) | data formatting | bytes 524288

commit v4 on v3

--- a/solution.py
+++ b/solution.py
@@ -19,11 +19,11 @@
 
 
 def kernel(
-    n, frames_n, x_tile, o_tile, p_tile, lag, direct, early,
-    tok, gain_hbm, wq_hbm, wo_hbm, keys, values, pos_hbm, pad,
+    n, frames_n, edges, o_tile, p_tile, lag, direct, early,
+    tok, gain_hbm, wq_hbm, wo_hbm, keys, values, pos_hbm, pad_hbm,
     out,
-    wq, wo, kg, vg, pos_col, gain, pos, raw, xg, qacc, qall, abuf, pbuf, rbuf,
-    q_sem, o_sem, own_sem, small_sem, kv_own, k_send, k_recv, v_send, v_recv,
+    wq, wo, kg, vg, pos_col, gain, pos, pad, raw, xg, qacc, qall, abuf, pbuf, rbuf,
+    weight_sem, own_sem, small_sem, kv_own, k_send, k_recv, v_send, v_recv,
     x_send, x_recv, p_send, p_recv,
 ):
     me_f = lax.axis_index("frame")
@@ -36,7 +36,7 @@
     phase_n = len(bits)
     k_order = bits
     v_order = bits[1::-1] + bits[2:] if phase_n > 1 else bits
-    n_x = width // x_tile
+    n_x = len(edges) - 1
     n_out = width // o_tile
     n_part = width // p_tile
     per_out = o_tile // p_tile
@@ -46,14 +46,8 @@
     middle = jnp.logical_and(has_left, has_right)
     low_half = 2 * me < n
 
-    def q_load(part):
-        window = pl.ds(part * x_tile, x_tile)
-        return pltpu.make_async_copy(wq_hbm.at[window], wq.at[window], q_sem.at[part])
-
-    def o_load(part):
-        depth = cols // 2
-        window = pl.ds(part * depth, depth)
-        return pltpu.make_async_copy(wo_hbm.at[window], wo.at[window], o_sem.at[part])
+    q_load = pltpu.make_async_copy(wq_hbm, wq, weight_sem.at[0])
+    o_load = pltpu.make_async_copy(wo_hbm, wo, weight_sem.at[1])
 
     def rows_of(block, count=1):
         return pl.ds(pl.multiple_of(block * rows, rows), count * rows)
@@ -61,6 +55,7 @@
     own_x = pltpu.make_async_copy(tok, raw, own_sem)
     own_gain = pltpu.make_async_copy(gain_hbm, gain, small_sem.at[0])
     own_pos = pltpu.make_async_copy(pos_hbm, pos, small_sem.at[1])
+    own_pad = pltpu.make_async_copy(pad_hbm, pad, small_sem.at[2])
     own_k = pltpu.make_async_copy(keys, kg.at[pl.ds(0, span)], kv_own.at[0])
     own_v = pltpu.make_async_copy(values, vg.at[pl.ds(0, span)], kv_own.at[1])
 
@@ -81,6 +76,7 @@
     own_x.start()
     own_gain.start()
     own_pos.start()
+    own_pad.start()
     own_k.start()
     own_v.start()
 
@@ -88,14 +84,13 @@
     own_gain.wait()
     own_k.wait()
     own_v.wait()
-    for part in range(n_x):
-        q_load(part).start()
-    for part in range(2):
-        o_load(part).start()
+    q_load.start()
+    o_load.start()
     hidden = raw[...].astype(jnp.float32)
     factor = lax.rsqrt(jnp.mean(hidden * hidden, axis=-1, keepdims=True) + epsilon)
     xg[rows_of(me), :] = (hidden * factor * gain[...]).astype(jnp.bfloat16)
     own_pos.wait()
+    own_pad.wait()
     pos_col[...] = jnp.broadcast_to(pos[...], (HEAD_DIM, n * rows)).T
 
     pl.semaphore_wait(
@@ -105,14 +100,15 @@
     def neighbour(side):
         return lax.rem(me + 1 - 2 * side + n, n)
 
+    def chunk_window(chunk):
+        return slice(edges[chunk], edges[chunk + 1])
+
     def token_copy(block, side, chunk):
-        window = pl.ds(chunk * x_tile, x_tile)
-        if not isinstance(chunk, int):
-            window = pl.ds(pl.multiple_of(chunk * x_tile, x_tile), x_tile)
+        window = chunk_window(chunk)
         return pltpu.make_async_remote_copy(
             src_ref=xg.at[rows_of(block), window],
             dst_ref=xg.at[rows_of(block), window],
-            send_sem=x_send.at[side, block],
+            send_sem=x_send,
             recv_sem=x_recv.at[block, chunk],
             device_id={"tensor": neighbour(side)},
             device_id_type=MESH,
@@ -127,14 +123,18 @@
         def _():
             token_copy(me, 1, chunk).start()
 
-    def frame_copy(ref, slot, bit, last, send, recv):
+    half = cols // 2
+
+    def frame_copy(ref, slot, bit, last, piece, send, recv):
         target = slot + bit
-        index = 0 if target & last else target % last + target // (2 * last) * last
+        window = pl.ds(piece * half, half)
+        index = target % last + target // (2 * last) * last
+        place = recv.at[0, 0] if target & last else recv.at[piece, index]
         return pltpu.make_async_remote_copy(
-            src_ref=ref.at[pl.ds(slot * span, span)],
-            dst_ref=ref.at[pl.ds(target * span, span)],
+            src_ref=ref.at[pl.ds(slot * span, span), window],
+            dst_ref=ref.at[pl.ds(target * span, span), window],
             send_sem=send,
-            recv_sem=recv.at[index],
+            recv_sem=place,
             device_id={"frame": flip(me_f, bit)},
             device_id_type=MESH,
         )
@@ -142,22 +142,24 @@
     def plan(ref, order, send, recv):
         steps, held = [], [0]
         last = order[-1]
+
+        def copies(slot, onto):
+            return [[frame_copy(ref, slot, bit, last, c, send, recv) for c in range(2)] for bit in onto]
+
         for p, bit in enumerate(order[:-1]):
             fresh = [slot + bit for slot in held]
             for slot in fresh:
-                arrival = frame_copy(ref, slot - bit, bit, last, send, recv)
-                onward = [
-                    frame_copy(ref, slot, later, last, send, recv) for later in order[p + 1:]
-                ]
-                steps.append((arrival, onward))
+                onward = copies(slot, order[p + 1:])
+                for piece, arrival in enumerate(copies(slot - bit, [bit])[0]):
+                    steps.append((arrival, [both[piece] for both in onward]))
             held = held + fresh
-        own = [frame_copy(ref, 0, bit, last, send, recv) for bit in order]
-        half = pl.ds(0, len(held) * span)
+        own = [copy for both in copies(0, order) for copy in both]
+        late = pl.ds(0, len(held) * span)
         rest = pltpu.make_async_remote_copy(
-            src_ref=ref.at[half],
-            dst_ref=ref.at[half],
+            src_ref=ref.at[late],
+            dst_ref=ref.at[late],
             send_sem=send,
-            recv_sem=recv.at[0],
+            recv_sem=recv.at[0, 0],
             device_id={"frame": flip(me_f, last)},
             device_id_type=MESH,
         )
@@ -169,20 +171,14 @@
         for copy in pair:
             copy.start()
     relays = list(zip(k_steps, v_steps))
-
-    def frame_step(pair):
-        for arrival, onward in pair:
-            arrival.wait_recv()
-            for copy in onward:
-                copy.start()
-
-    def frame_steps(chunk):
-        if chunk < n_x - 2:
-            for pair in relays[chunk:chunk + 1]:
-                frame_step(pair)
-        if chunk == n_x - 1:
-            for pair in relays[max(n_x - 2, 0):]:
-                frame_step(pair)
+    cuts = [0] + [len(relays) * (i + 1) // (n_x + 2) for i in range(n_x)] + [len(relays)]
+
+    def frame_steps(turn):
+        for pair in relays[cuts[turn]:cuts[turn + 1]]:
+            for arrival, onward in pair:
+                arrival.wait_recv()
+                for copy in onward:
+                    copy.start()
 
     def frames_done():
         k_rest.wait_recv()
@@ -197,14 +193,14 @@
                 owner = flip(owner, bit)
         pieces.append(slot_of + owner * span)
     frame_index = jnp.concatenate(pieces, axis=1)
-    visible_frames = frame_index < frames_n * span - pad[0]
+    visible_frames = frame_index < frames_n * span - pad[...]
 
     scale = HEAD_DIM ** (-0.5)
 
-    def q_first(block, count, chunk):
-        window = slice(chunk * x_tile, (chunk + 1) * x_tile)
+    def q_step(block, count, place, chunk):
+        window = chunk_window(chunk)
         at = rows_of(block, count)
-        held = pl.ds(0, count * rows)
+        held = rows_of(place, count)
         product = jnp.dot(xg[at, window], wq[window, :], preferred_element_type=jnp.float32)
         if chunk > 0:
             product = qacc[held, :] + product
@@ -212,27 +208,6 @@
             qacc[held, :] = product
         else:
             qall[at, :] = (product * scale).astype(jnp.bfloat16)
-
-    def q_step(block, place, chunk):
-        window = pl.ds(pl.multiple_of(chunk * x_tile, x_tile), x_tile)
-        held = pl.ds(place * rows, rows)
-        if not isinstance(place, int):
-            held = rows_of(place)
-        product = jnp.dot(
-            xg[rows_of(block), window], wq[window, :], preferred_element_type=jnp.float32
-        )
-
-        @pl.when(chunk == 0)
-        def _():
-            qacc[held, :] = product
-
-        @pl.when(chunk > 0)
-        def _():
-            qacc[held, :] += product
-
-        @pl.when(chunk == n_x - 1)
-        def _():
-            qall[rows_of(block), :] = (qacc[held, :] * scale).astype(jnp.bfloat16)
 
     def attend(block, count):
         at = rows_of(block, count)
@@ -290,42 +265,42 @@
                 abuf[at, :], wo[:, window], preferred_element_type=jnp.float32
             ).astype(jnp.bfloat16)
 
-            @pl.when(index > 0)
-            def _():
-                send(lax.rem(tile + n_out - 1, n_out))
-
+            if send is not None:
+                send(tile)
             return 0
 
         lax.fori_loop(0, n_out, body, 0)
-        send((first_tile + n_out - 1) % n_out)
 
     def parts_of(tile):
         return [tile * per_out + part for part in range(per_out)]
 
     def drain_inputs():
-        def drain_body(block, _):
-            for side, sent in ((0, has_right & (block <= me)), (1, has_left & (block >= me))):
-                @pl.when(sent)
-                def _():
-                    pltpu.make_async_remote_copy(
-                        src_ref=xg.at[rows_of(block)],
-                        dst_ref=xg.at[rows_of(block)],
-                        send_sem=x_send.at[side, block],
-                        recv_sem=x_recv.at[block, 0],
-                        device_id={"tensor": neighbour(side)},
-                        device_id_type=MESH,
-                    ).wait_send()
-
-            return 0
-
-        lax.fori_loop(0, n, drain_body, 0)
+        def drain_tokens(count):
+            sent = pl.ds(0, count * rows)
+            pltpu.make_async_remote_copy(
+                src_ref=xg.at[sent],
+                dst_ref=xg.at[sent],
+                send_sem=x_send,
+                recv_sem=x_recv.at[0, 0],
+                device_id={"tensor": neighbour(0)},
+                device_id_type=MESH,
+            ).wait_send()
+
+        @pl.when(middle)
+        def _():
+            drain_tokens(n + 1)
+
+        @pl.when(jnp.logical_not(middle))
+        def _():
+            drain_tokens(1)
+
         others = pl.ds(0, (frames_n - 1) * span)
         for ref, send, recv in ((kg, k_send, k_recv), (vg, v_send, v_recv)):
             pltpu.make_async_remote_copy(
                 src_ref=ref.at[others],
                 dst_ref=ref.at[others],
                 send_sem=send,
-                recv_sem=recv.at[0],
+                recv_sem=recv.at[0, 0],
                 device_id={"frame": flip(me_f, bits[0])},
                 device_id_type=MESH,
             ).wait_send()
@@ -337,32 +312,29 @@
         leaving = 1 - arriving
         near = me + heading
         first = jnp.minimum(me, near)
+        frame_steps(0)
+        q_load.wait()
         for chunk in range(n_x):
-            q_load(chunk).wait()
             token_copy(near, arriving, chunk).wait_recv()
-            q_first(first, 2, chunk)
-            frame_steps(chunk)
+            q_step(first, 2, 0, chunk)
+            frame_steps(chunk + 1)
         frames_done()
-        attend(first, 2)
-        for part in range(2):
-            o_load(part).wait()
+        attend(near, 1)
+        o_load.wait()
 
 
         def send_near(tile):
             for part in parts_of(tile):
                 part_copy(near, leaving, part).start()
 
-        project(first, 2, 0, send_near)
+        project(near, 1, 0, send_near)
 
         def stage_body(stage, _):
             block = me + heading * stage
 
-            def chunk_body(chunk, _):
+            for chunk in range(n_x):
                 token_copy(block, arriving, chunk).wait_recv()
-                q_step(block, 0, chunk)
-                return 0
-
-            lax.fori_loop(0, n_x, chunk_body, 0)
+                q_step(block, 1, 0, chunk)
             attend(block, 1)
 
             def send_block(tile):
@@ -374,6 +346,8 @@
             return 0
 
         lax.fori_loop(2, n, stage_body, 0)
+        attend(me, 1)
+        project(me, 1, 0, None)
         drain_inputs()
 
         def sum_body(tile, _):
@@ -401,16 +375,21 @@
 
     @pl.when(middle)
     def _():
+        frame_steps(0)
+        q_load.wait()
         for chunk in range(n_x):
-            q_load(chunk).wait()
             for side, block in ((0, me - 1), (1, me + 1)):
                 token_copy(block, side, chunk).wait_recv()
                 token_copy(block, side, chunk).start()
-            q_first(me - 1, 3, chunk)
-            frame_steps(chunk)
+            q_step(me - 1, 3, 0, chunk)
+            frame_steps(chunk + 1)
+
+        def near_attend():
+            frames_done()
+            attend(me - 1, 3)
 
         def stage_body(stage, _):
-            def chunk_body(chunk, _):
+            for chunk in range(n_x):
                 def side_body(side, _):
                     block = me - stage + 2 * side * stage
 
@@ -418,28 +397,36 @@
                     def _():
                         token_copy(block, side, chunk).wait_recv()
                         token_copy(block, side, chunk).start()
-                        q_step(block, side, chunk)
+                        q_step(block, 1, side, chunk)
 
                     return 0
 
                 lax.fori_loop(0, 2, side_body, 0)
+                if chunk == 0:
+                    pl.when(stage == 2)(near_attend)
+
+            def attend_body(side, _):
+                block = me - stage + 2 * side * stage
+
+                @pl.when(jnp.logical_and(block >= 0, block < n))
+                def _():
+                    attend(block, 1)
+
                 return 0
 
-            lax.fori_loop(0, n_x, chunk_body, 0)
-            return 0
-
+            lax.fori_loop(0, 2, attend_body, 0)
+            return 0
+
+        if n == 3:
+            near_attend()
         lax.fori_loop(2, n - 1, stage_body, 0)
-        frames_done()
         groups = max(1, n * rows // HEAD_DIM)
         while n % groups:
             groups -= 1
         count = n // groups
-        for part in range(2):
-            o_load(part).wait()
+        o_load.wait()
 
         def group_body(group, _):
-            attend(group * count, count)
-
             def send_started(tile):
                 last = group == groups - 1
                 for part in parts_of(tile):
@@ -529,10 +516,12 @@
     rows, seqs, width = tokens.shape
     cols = query_weight.shape[1]
     span = cache_keys.shape[0]
-    x_tile = divisor(width, 1024)
+    unit = divisor(width, 256)
+    shares = (6, 5, 3, 2)
+    edges = [width // unit * sum(shares[:i]) // sum(shares) * unit for i in range(len(shares) + 1)]
     o_tile = divisor(width, 512)
     p_tile = divisor(o_tile, 512)
-    n_x = width // x_tile
+    n_x = len(shares)
     n_part = width // p_tile
     lag = max(1, 5 * n_part // 8)
     direct = n_part if n > 2 else 0
@@ -542,9 +531,9 @@
     bf16 = jnp.bfloat16
     dma = pltpu.SemaphoreType.DMA
     result = pl.pallas_call(
-        functools.partial(kernel, n, frames_n, x_tile, o_tile, p_tile, lag, direct, early),
+        functools.partial(kernel, n, frames_n, edges, o_tile, p_tile, lag, direct, early),
         out_shape=pltpu.VMEM((rows, width), bf16),
-        in_specs=[hbm, hbm, hbm, hbm, hbm, hbm, hbm, pl.BlockSpec(memory_space=pltpu.SMEM)],
+        in_specs=[hbm] * 8,
         out_specs=vmem,
         scratch_shapes=[
             pltpu.VMEM(query_weight.shape, bf16),
@@ -554,23 +543,23 @@
             pltpu.VMEM((n * rows, HEAD_DIM), jnp.int32),
             pltpu.VMEM((1, width), jnp.float32),
             pltpu.VMEM((1, n * rows), jnp.int32),
+            pltpu.VMEM((1, 1), jnp.int32),
             pltpu.VMEM((rows, width), bf16),
-            pltpu.VMEM((n * rows, width), bf16),
+            pltpu.VMEM(((n + 1) * rows, width), bf16),
             pltpu.VMEM((3 * rows, cols), jnp.float32),
             pltpu.VMEM((n * rows, cols), bf16),
             pltpu.VMEM((n * rows, cols), bf16),
             pltpu.VMEM((n * rows, width), bf16),
             pltpu.VMEM((2, n * rows, width), bf16),
-            dma((n_x,)),
             dma((2,)),
             dma(()),
-            dma((2,)),
+            dma((3,)),
             dma((2,)),
             dma(()),
-            dma((frames_n // 2,)),
+            dma((2, frames_n // 2)),
             dma(()),
-            dma((frames_n // 2,)),
-            dma((2, n)),
+            dma((2, frames_n // 2)),
+            dma(()),
             dma((n, n_x)),
             dma(()),
             dma((n + 1, n_part)),
@@ -584,7 +573,7 @@
         cache_keys.reshape(span, cols),
         cache_values.reshape(span, cols),
         token_pos.reshape(1, n * rows),
-        frame_pad,
+        frame_pad.reshape(1, 1),
     )
     return result.reshape(rows, seqs, width)
 

time: 38 us -> 37.3 us (0.982)
  Pallas kernels: 36.2 us -> 35.7 us
    pallas_call x1, Pallas kernels: 36.2 us -> 35.7 us  [per_device(): pl.pallas_call(functools.partial(kernel, n, frames_n, edges, o_tile, p_ti...]
where the time goes in v4:
time: 37.3 us; the launch traced here: 37.1 us
  Pallas kernels  35.7 us (96%)
  local copies, waits for them, and re-layouts  0.71 us (2%)
  between operations  0.66 us (2%)
    pallas_call x1, Pallas kernels, per_device(): pl.pallas_call(functools.partial(kernel, n, frames_n, edges, o_tile, p_ti...  35.7 us

profile of v4, /device:TPU:11, one launch (start us, length us, event | category | flops | bytes accessed | tf_op | source)
XLA Modules:
  0.0 37.1 jit_solution(13126629755904540287)
XLA Ops:
  0.7 35.7 %shard_map.82 = bf16[32,4096]{1,0:T(8,128)(2,1)S(1)} custom-call(bf16[32,4096]{1,0:T(8,128)(2,1)} %bitcast.9, f32[1,4096]{1,0:T(1,128)} %bitcast.12, bf16[4096,1024]{1,0:T(8,128)(2,1)} %wq_hbm.1, bf16[1024,4096]{1,0:T(8,128)(2,1)} %wo_hbm.1, bf16[48,1024]{1,0:T(8,128)(2,1)} %bitcast.10, bf16[48,1024]{1,0:T(8,128)(2,1)} %bitcast.11, s32[1,128]{1,0:T(1,128)} %bitcast.13, ...), custom_call_target="tpu_custom_call" | custom-call | tf_op jit(solution)/shard_map/pallas_call | solution.py:533
  36.4 0.7 %copy.10 = bf16[32,1,4096]{2,0,1:T(8,128)(2,1)} copy(bf16[32,1,4096]{2,0,1:T(8,128)(2,1)S(1)} %bitcast.8) | data formatting | bytes 524288

commit v5 on v4

--- a/solution.py
+++ b/solution.py
@@ -19,7 +19,7 @@
 
 
 def kernel(
-    n, frames_n, edges, o_tile, p_tile, lag, direct, early,
+    n, frames_n, edges, o_tile, p_tile, lag, direct, early, carry, defer,
     tok, gain_hbm, wq_hbm, wo_hbm, keys, values, pos_hbm, pad_hbm,
     out,
     wq, wo, kg, vg, pos_col, gain, pos, pad, raw, xg, qacc, qall, abuf, pbuf, rbuf,
@@ -41,6 +41,7 @@
     n_part = width // p_tile
     per_out = o_tile // p_tile
     chained = n_part - direct
+    alone = n_part - carry
     has_left = me > 0
     has_right = me < n - 1
     middle = jnp.logical_and(has_left, has_right)
@@ -222,9 +223,7 @@
         ]
         scores = [jnp.where(visible, score, masked_score) for score in scores]
         highest = [jnp.max(score, axis=-1, keepdims=True) for score in scores]
-        weights = [
-            jnp.where(visible, jnp.exp(score - top), 0.0) for score, top in zip(scores, highest)
-        ]
+        weights = [jnp.exp(score - top) for score, top in zip(scores, highest)]
         totals = [jnp.sum(weight, axis=-1, keepdims=True) for weight in weights]
         gathered = [
             jnp.dot(weight.astype(jnp.bfloat16), vg[:, window], preferred_element_type=jnp.float32)
@@ -270,6 +269,14 @@
             return 0
 
         lax.fori_loop(0, n_out, body, 0)
+
+    def add_part(block, side, tile):
+        at = rows_of(block)
+        window = part_window(tile)
+        part_here(block, side, tile).wait_recv()
+        pbuf[at, window] = (
+            pbuf[at, window].astype(jnp.float32) + rbuf[side, at, window].astype(jnp.float32)
+        ).astype(jnp.bfloat16)
 
     def parts_of(tile):
         return [tile * per_out + part for part in range(per_out)]
@@ -322,10 +329,11 @@
         attend(near, 1)
         o_load.wait()
 
-
         def send_near(tile):
             for part in parts_of(tile):
-                part_copy(near, leaving, part).start()
+                @pl.when(part < n_part - defer)
+                def _():
+                    part_copy(near, leaving, part).start()
 
         project(near, 1, 0, send_near)
 
@@ -340,12 +348,19 @@
             def send_block(tile):
                 for part in parts_of(tile):
                     far = jnp.logical_and(stage == n - 1, part >= chained)
+
+                    @pl.when(far & has_left & (part >= alone))
+                    def _():
+                        add_part(block, 0, part)
+
                     part_copy(block, leaving, part, far).start()
 
             project(block, 1, 0, send_block)
             return 0
 
         lax.fori_loop(2, n, stage_body, 0)
+        for part in range(n_part - defer, n_part):
+            part_copy(near, leaving, part).start()
         attend(me, 1)
         project(me, 1, 0, None)
         drain_inputs()
@@ -434,7 +449,10 @@
                     def _():
                         part_copy(n - 1, 0, part).start()
 
-                    @pl.when((me == n - 2) & (group == 0) & (part >= chained))
+                    carried = part >= alone
+                    begins = jnp.where(carried, me == n - 3, me == n - 2)
+
+                    @pl.when(begins & (group == 0) & (part >= chained))
                     def _():
                         part_copy(0, 1, part).start()
 
@@ -443,14 +461,13 @@
 
         lax.fori_loop(0, groups, group_body, 0)
 
+        @pl.when(me == n - 2)
+        def _():
+            for part in range(alone, n_part):
+                part_copy(0, 0, part).start()
+
         def relay(block, side, tile):
-            at = rows_of(block)
-            window = part_window(tile)
-            part_here(block, side, tile).wait_recv()
-            pbuf[at, window] = (
-                pbuf[at, window].astype(jnp.float32)
-                + rbuf[side, at, window].astype(jnp.float32)
-            ).astype(jnp.bfloat16)
+            add_part(block, side, tile)
             part_copy(block, side, tile).start()
 
         def relay_body(index, _):
@@ -468,7 +485,8 @@
                     relay(block, side, tile)
 
                 far = index - (n - 3) * n_part - early
-                beside = jnp.where(side == 0, me == 1, me == n - 2)
+                carried = chained + far >= alone
+                beside = jnp.where(side == 0, me == 1, (me == n - 2) | (carried & (me == n - 3)))
 
                 @pl.when((far >= 0) & (far < direct) & jnp.logical_not(beside))
                 def _():
@@ -526,12 +544,14 @@
     lag = max(1, 5 * n_part // 8)
     direct = n_part if n > 2 else 0
     early = -(3 * n_part // 8)
+    carry = 3 * n_part // 8 if n > 3 else 0
+    defer = n_part // 8 if n > 3 else 0
     hbm = pl.BlockSpec(memory_space=pltpu.HBM)
     vmem = pl.BlockSpec(memory_space=pltpu.VMEM)
     bf16 = jnp.bfloat16
     dma = pltpu.SemaphoreType.DMA
     result = pl.pallas_call(
-        functools.partial(kernel, n, frames_n, edges, o_tile, p_tile, lag, direct, early),
+        functools.partial(kernel, n, frames_n, edges, o_tile, p_tile, lag, direct, early, carry, defer),
         out_shape=pltpu.VMEM((rows, width), bf16),
         in_specs=[hbm] * 8,
         out_specs=vmem,

time: 37.3 us -> 36.5 us (0.979)
  Pallas kernels: 35.7 us -> 34.7 us
    pallas_call x1, Pallas kernels: 35.7 us -> 34.7 us  [per_device(): pl.pallas_call(functools.partial(kernel, n, frames_n, edges, o_tile, p_ti...]
where the time goes in v5:
time: 36.5 us; the launch traced here: 36 us
  Pallas kernels  34.7 us (95%)
  local copies, waits for them, and re-layouts  0.71 us (2%)
  between operations  0.66 us (2%)
    pallas_call x1, Pallas kernels, per_device(): pl.pallas_call(functools.partial(kernel, n, frames_n, edges, o_tile, p_ti...  34.7 us

profile of v5, /device:TPU:11, one launch (start us, length us, event | category | flops | bytes accessed | tf_op | source)
XLA Modules:
  0.0 36.0 jit_solution(5740065578980095345)
XLA Ops:
  0.7 34.7 %shard_map.82 = bf16[32,4096]{1,0:T(8,128)(2,1)S(1)} custom-call(bf16[32,4096]{1,0:T(8,128)(2,1)} %bitcast.9, f32[1,4096]{1,0:T(1,128)} %bitcast.12, bf16[4096,1024]{1,0:T(8,128)(2,1)} %wq_hbm.1, bf16[1024,4096]{1,0:T(8,128)(2,1)} %wo_hbm.1, bf16[48,1024]{1,0:T(8,128)(2,1)} %bitcast.10, bf16[48,1024]{1,0:T(8,128)(2,1)} %bitcast.11, s32[1,128]{1,0:T(1,128)} %bitcast.13, ...), custom_call_target="tpu_custom_call" | custom-call | tf_op jit(solution)/shard_map/pallas_call | solution.py:553
  35.3 0.7 %copy.10 = bf16[32,1,4096]{2,0,1:T(8,128)(2,1)} copy(bf16[32,1,4096]{2,0,1:T(8,128)(2,1)S(1)} %bitcast.8) | data formatting | bytes 524288

commit v6 on v5

--- a/solution.py
+++ b/solution.py
@@ -104,13 +104,14 @@
     def chunk_window(chunk):
         return slice(edges[chunk], edges[chunk + 1])
 
-    def token_copy(block, side, chunk):
+    def token_copy(block, side, chunk, receiver=None):
+        receiver = neighbour(side) if receiver is None else receiver
         window = chunk_window(chunk)
         return pltpu.make_async_remote_copy(
             src_ref=xg.at[rows_of(block), window],
             dst_ref=xg.at[rows_of(block), window],
             send_sem=x_send,
-            recv_sem=x_recv.at[block, chunk],
+            recv_sem=x_recv.at[block - (block > receiver).astype(jnp.int32), chunk],
             device_id={"tensor": neighbour(side)},
             device_id_type=MESH,
         )
@@ -130,7 +131,7 @@
         target = slot + bit
         window = pl.ds(piece * half, half)
         index = target % last + target // (2 * last) * last
-        place = recv.at[0, 0] if target & last else recv.at[piece, index]
+        place = recv.at[0] if target & last else recv.at[2 * index - 1 + piece]
         return pltpu.make_async_remote_copy(
             src_ref=ref.at[pl.ds(slot * span, span), window],
             dst_ref=ref.at[pl.ds(target * span, span), window],
@@ -160,7 +161,7 @@
             src_ref=ref.at[late],
             dst_ref=ref.at[late],
             send_sem=send,
-            recv_sem=recv.at[0, 0],
+            recv_sem=recv.at[0],
             device_id={"frame": flip(me_f, last)},
             device_id_type=MESH,
         )
@@ -235,15 +236,31 @@
     def part_window(tile):
         return pl.ds(pl.multiple_of(tile * p_tile, p_tile), p_tile)
 
+    def whole_slot(receiver):
+        inner = jnp.where(2 * receiver < n, 0, 1)
+        return jnp.where(receiver == 0, 1, jnp.where(receiver == n - 1, 0, inner))
+
+    def whole_wait():
+        slot = whole_slot(me)
+        pltpu.make_async_remote_copy(
+            src_ref=pbuf.at[rows_of(me)],
+            dst_ref=rbuf.at[slot, rows_of(me)],
+            send_sem=p_send,
+            recv_sem=p_recv.at[n * n_part],
+            device_id={"tensor": neighbour(0)},
+            device_id_type=MESH,
+        ).wait_recv()
+
     def part_move(block, side, tile, far, receiver):
         slot = jnp.where(far, 1 - side, side)
         towards = jnp.where(far, block, neighbour(side))
         receiver = towards if receiver is None else receiver
+        whole = (block == receiver) & (slot == whole_slot(receiver))
         return pltpu.make_async_remote_copy(
             src_ref=pbuf.at[rows_of(block), part_window(tile)],
             dst_ref=rbuf.at[slot, rows_of(block), part_window(tile)],
             send_sem=p_send,
-            recv_sem=p_recv.at[jnp.where((slot == 1) & (block == receiver), n, block), tile],
+            recv_sem=p_recv.at[jnp.where(whole, n * n_part, block * n_part + tile)],
             device_id={"tensor": towards},
             device_id_type=MESH,
         )
@@ -307,7 +324,7 @@
                 src_ref=ref.at[others],
                 dst_ref=ref.at[others],
                 send_sem=send,
-                recv_sem=recv.at[0, 0],
+                recv_sem=recv.at[0],
                 device_id={"frame": flip(me_f, bits[0])},
                 device_id_type=MESH,
             ).wait_send()
@@ -322,7 +339,7 @@
         frame_steps(0)
         q_load.wait()
         for chunk in range(n_x):
-            token_copy(near, arriving, chunk).wait_recv()
+            token_copy(near, arriving, chunk, me).wait_recv()
             q_step(first, 2, 0, chunk)
             frame_steps(chunk + 1)
         frames_done()
@@ -341,7 +358,7 @@
             block = me + heading * stage
 
             for chunk in range(n_x):
-                token_copy(block, arriving, chunk).wait_recv()
+                token_copy(block, arriving, chunk, me).wait_recv()
                 q_step(block, 1, 0, chunk)
             attend(block, 1)
 
@@ -365,9 +382,10 @@
         project(me, 1, 0, None)
         drain_inputs()
 
+        whole_wait()
+
         def sum_body(tile, _):
             window = part_window(tile)
-            part_here(me, arriving, tile).wait_recv()
             total = pbuf[rows_of(me), window].astype(jnp.float32)
             total = total + rbuf[arriving, rows_of(me), window].astype(jnp.float32)
 
@@ -394,7 +412,7 @@
         q_load.wait()
         for chunk in range(n_x):
             for side, block in ((0, me - 1), (1, me + 1)):
-                token_copy(block, side, chunk).wait_recv()
+                token_copy(block, side, chunk, me).wait_recv()
                 token_copy(block, side, chunk).start()
             q_step(me - 1, 3, 0, chunk)
             frame_steps(chunk + 1)
@@ -410,7 +428,7 @@
 
                     @pl.when(jnp.logical_and(block >= 0, block < n))
                     def _():
-                        token_copy(block, side, chunk).wait_recv()
+                        token_copy(block, side, chunk, me).wait_recv()
                         token_copy(block, side, chunk).start()
                         q_step(block, 1, side, chunk)
 
@@ -500,11 +518,14 @@
         behind = jnp.minimum(me, n - 1 - me) * n_part
         lax.fori_loop(jnp.minimum(behind, (n - 3) * n_part + early), (n - 1) * n_part + lag, relay_body, 0)
 
+        whole_wait()
+        slot = whole_slot(me)
+
         def sum_body(tile, _):
             window = part_window(tile)
+            part_here(me, 1 - slot, tile).wait_recv()
             total = pbuf[rows_of(me), window].astype(jnp.float32)
             for side in range(2):
-                part_here(me, side, tile).wait_recv()
                 total = total + rbuf[side, rows_of(me), window].astype(jnp.float32)
             out[:, window] = total.astype(jnp.bfloat16)
             return 0
@@ -517,7 +538,7 @@
         src_ref=pbuf.at[others],
         dst_ref=rbuf.at[0, others],
         send_sem=p_send,
-        recv_sem=p_recv.at[0, 0],
+        recv_sem=p_recv.at[0],
         device_id={"tensor": neighbour(0)},
         device_id_type=MESH,
     ).wait_send()
@@ -543,7 +564,7 @@
     n_part = width // p_tile
     lag = max(1, 5 * n_part // 8)
     direct = n_part if n > 2 else 0
-    early = -(3 * n_part // 8)
+    early = -(2 * n_part // 8)
     carry = 3 * n_part // 8 if n > 3 else 0
     defer = n_part // 8 if n > 3 else 0
     hbm = pl.BlockSpec(memory_space=pltpu.HBM)
@@ -576,13 +597,13 @@
             dma((3,)),
             dma((2,)),
             dma(()),
-            dma((2, frames_n // 2)),
+            dma((frames_n - 1,)),
             dma(()),
-            dma((2, frames_n // 2)),
+            dma((frames_n - 1,)),
             dma(()),
-            dma((n, n_x)),
+            dma((n - 1, n_x)),
             dma(()),
-            dma((n + 1, n_part)),
+            dma((n * n_part + 1,)),
         ],
         compiler_params=pltpu.CompilerParams(collective_id=0, has_side_effects=True),
     )(

time: 36.5 us -> 36.3 us (level)
  no operation moved by 1% of the time
where the time goes in v6:
time: 36.3 us; the launch traced here: 35.8 us
  Pallas kernels  34.5 us (95%)
  local copies, waits for them, and re-layouts  0.71 us (2%)
  between operations  0.66 us (2%)
    pallas_call x1, Pallas kernels, per_device(): pl.pallas_call(functools.partial(kernel, n, frames_n, edges, o_tile, p_ti...  34.5 us

profile of v6, /device:TPU:11, one launch (start us, length us, event | category | flops | bytes accessed | tf_op | source)
XLA Modules:
  0.0 35.8 jit_solution(3894470604887184012)
XLA Ops:
  0.7 34.5 %shard_map.82 = bf16[32,4096]{1,0:T(8,128)(2,1)S(1)} custom-call(bf16[32,4096]{1,0:T(8,128)(2,1)} %bitcast.9, f32[1,4096]{1,0:T(1,128)} %bitcast.12, bf16[4096,1024]{1,0:T(8,128)(2,1)} %wq_hbm.1, bf16[1024,4096]{1,0:T(8,128)(2,1)} %wo_hbm.1, bf16[48,1024]{1,0:T(8,128)(2,1)} %bitcast.10, bf16[48,1024]{1,0:T(8,128)(2,1)} %bitcast.11, s32[1,128]{1,0:T(1,128)} %bitcast.13, ...), custom_call_target="tpu_custom_call" | custom-call | tf_op jit(solution)/shard_map/pallas_call | solution.py:574
  35.1 0.7 %copy.10 = bf16[32,1,4096]{2,0,1:T(8,128)(2,1)} copy(bf16[32,1,4096]{2,0,1:T(8,128)(2,1)S(1)} %bitcast.8) | data formatting | bytes 524288
